TPU v7x, 32 devices: a whole 2x2x4 slice. The times are simulated.
32 devices in a mesh: groups: 2 (over y), row: 4 (over z), col: 2 (over x), sub: 2 (over core).
Axes of the slice: x: 2, y: 2, z: 4, core: 2. Of those that a mesh axis runs over, the one named last changes fastest.
Arguments:
- stream_in: bfloat16 [4096, 5376], P(('groups', 'row'), ('col', 'sub')), parts along dimension 0, may hold values from -6 to 6
- in_gain: float32 [5376], replicated, may hold values from 0.1 to 1.9
- query_weight: bfloat16 [5376, 4096], P('row', ('col', 'sub')), may hold values from -0.078125 to 0.078125
- key_matrix: bfloat16 [5376, 2048], P('row', ('col', 'sub')), may hold values from -0.078125 to 0.078125
- value_matrix: bfloat16 [5376, 2048], P('row', ('col', 'sub')), may hold values from -0.078125 to 0.078125
- query_gain: float32 [128], replicated, may hold values from 0.45 to 10, as said below
- key_norm_gain: float32 [128], replicated, may hold values from 0.45 to 10, as said below
- output_weight: bfloat16 [4096, 5376], P('row', ('col', 'sub')), may hold values from -3 to 3
- post_gain: float32 [5376], P(('col', 'sub')), may hold values from 0.1 to 1.9
Outputs:
- stream_out: bfloat16 [4096, 5376], P(('groups', 'row'), ('col', 'sub')), parts along dimension 0
There are 2 independent parts, one for each index of `groups`. A program takes and returns all parts, laid end to end along the dimension named above; an argument that names none is the same for every part. Nothing has to cross between parts.
Inputs may be any that keep to these rules, and one draw needn't show every extreme that they name: `query_gain`: positive. `key_norm_gain`: positive.
All inputs are finite; a program needn't handle non-finite values.
Results may differ from a plain program's by a relative error of at most 0.014.
The roundings to bfloat16 on the way count: a program that leaves them out, or rounds other values in their place, can miss the bound.
Values may be sent and summed in bfloat16 or wider, within the bound.
A program may use at most 128 MiB of HBM per device.

v0:
```python
import jax
import jax.numpy as jnp
from jax import lax
from jax.sharding import PartitionSpec as P

MODEL_WIDTH = 5376
QUERY_HEAD_COUNT = 32
WINDOW_LENGTH = 1024


EPSILON = 1e-06


def shifted(x, axis, by):
    count = lax.axis_size(axis)
    pairs = [(i, i + by) for i in range(count) if 0 <= i + by < count]
    return lax.ppermute(x, axis, pairs)


def root_mean_scale(values, gain):
    return values * lax.rsqrt(jnp.mean(values * values, axis=-1, keepdims=True) + EPSILON) * gain


def apply_rotary(tensor, token_positions):
    half_dim = tensor.shape[-1] // 2
    inverse = 10000.0 ** (-(jnp.arange(half_dim, dtype=jnp.float32) * 2.0) / tensor.shape[-1])
    angles = token_positions[:, None] * inverse[None, :]
    cosine = jnp.cos(angles)[:, None, :]
    sine_part = jnp.sin(angles)[:, None, :]
    first_half = tensor[..., :half_dim]
    second_half = tensor[..., half_dim:]
    return jnp.concatenate(
        [
            first_half * cosine - second_half * sine_part,
            second_half * cosine + first_half * sine_part,
        ],
        axis=-1,
    )


def on_device(
    stream_in,
    in_gain,
    query_weight,
    key_matrix,
    value_matrix,
    query_gain,
    key_norm_gain,
    output_weight,
    post_gain,
):
    token_rows = lax.all_gather(stream_in, ("col", "sub"), axis=1, tiled=True)
    tokens = token_rows.shape[0]
    normed = root_mean_scale(token_rows.astype(jnp.float32), in_gain).astype(jnp.bfloat16)

    def add_panel(panel_piece):
        return jnp.dot(normed, panel_piece, preferred_element_type=jnp.float32)

    query_proj = add_panel(lax.all_gather(query_weight, "row", axis=0, tiled=True))
    projected_keys = add_panel(lax.all_gather(key_matrix, "row", axis=0, tiled=True))
    projected_values = add_panel(lax.all_gather(value_matrix, "row", axis=0, tiled=True))
    head_size = query_gain.shape[0]
    query_heads = query_weight.shape[1] // head_size
    pair_heads = key_matrix.shape[1] // head_size
    group_count = query_heads // pair_heads
    scale_factor = float(MODEL_WIDTH // QUERY_HEAD_COUNT) ** (-0.5)
    row_index = lax.axis_index("row")
    query_places = row_index * tokens + jnp.arange(tokens, dtype=jnp.int32)
    query_rot = apply_rotary(
        root_mean_scale(query_proj.reshape(tokens, query_heads, head_size), query_gain),
        query_places.astype(jnp.float32),
    ).astype(jnp.bfloat16)
    rotary_keys = apply_rotary(
        root_mean_scale(projected_keys.reshape(tokens, pair_heads, head_size), key_norm_gain),
        query_places.astype(jnp.float32),
    ).astype(jnp.bfloat16)
    keys_flat = rotary_keys.reshape(tokens, pair_heads * head_size)
    values_flat = projected_values.astype(jnp.bfloat16)
    shards_back = min(WINDOW_LENGTH // tokens, lax.axis_size("row") - 1)
    band_length = (shards_back + 1) * tokens
    key_parts = [keys_flat]
    value_parts = [values_flat]
    for offset in range(1, shards_back + 1):
        keys_prior, values_prior = shifted((keys_flat, values_flat), "row", offset)
        key_parts = [keys_prior] + key_parts
        value_parts = [values_prior] + value_parts
    keys_band = jnp.concatenate(key_parts, axis=0)
    values_band = jnp.concatenate(value_parts, axis=0)
    key_places = (row_index - shards_back) * tokens + jnp.arange(band_length, dtype=jnp.int32)
    distance = query_places[:, None] - key_places[None, :]
    visible = (distance >= 0) & (distance < WINDOW_LENGTH) & (key_places[None, :] >= 0)
    grouped = query_rot.reshape(tokens, pair_heads, group_count, head_size)
    scores = (
        jnp.einsum(
            "qhgd,shd->hgqs",
            grouped,
            keys_band.reshape(band_length, pair_heads, head_size),
            preferred_element_type=jnp.float32,
        )
        * scale_factor
    )
    scores = jnp.where(visible, scores, -1e30)
    row_max = jnp.max(scores, axis=-1, keepdims=True)
    exponent = jnp.exp(scores - row_max)
    weights = (exponent / jnp.sum(exponent, axis=-1, keepdims=True)).astype(jnp.bfloat16)
    attended = jnp.einsum(
        "hgqs,shd->qhgd",
        weights,
        values_band.reshape(band_length, pair_heads, head_size),
        preferred_element_type=jnp.float32,
    )
    heads_out = attended.reshape(tokens, query_heads * head_size).astype(jnp.bfloat16)
    head_rows = lax.all_gather(heads_out, ("col", "sub"), axis=1, tiled=True)
    branch = jnp.dot(
        head_rows,
        lax.all_gather(output_weight, "row", axis=0, tiled=True),
        preferred_element_type=jnp.float32,
    )
    squares = lax.psum(jnp.sum(branch * branch, axis=-1), ("col", "sub"))
    scaled = branch * lax.rsqrt(squares[:, None] / MODEL_WIDTH + EPSILON) * post_gain
    return (stream_in.astype(jnp.float32) + scaled).astype(jnp.bfloat16)


def solution(mesh):
    placed = (
        P(("groups", "row"), ("col", "sub")),
        P(),
        P("row", ("col", "sub")),
        P("row", ("col", "sub")),
        P("row", ("col", "sub")),
        P(),
        P(),
        P("row", ("col", "sub")),
        P(("col", "sub")),
    )
    return jax.shard_map(
        on_device,
        mesh=mesh,
        in_specs=placed,
        out_specs=P(("groups", "row"), ("col", "sub")),
        check_vma=False,
    )
```

profile of v0, /device:TPU:22, one launch (start us, length us, event | category | flops | bytes accessed | tf_op | source)
XLA Modules:
  0.0 757.4 jit_solution(18262040499544532429)
XLA Ops:
  6.5 0.7 all-gather.7.cloned.1.call-update
  7.3 0.7 all-gather.11.cloned.1.call-update
  10.0 1.0 multiply_cosine_fusion
  11.0 39.9 %all-gather.7.cloned.1.call-done = bf16[512,5376]{0,1:T(8,128)(2,1)} async-done(((bf16[512,1344]{0,1:T(8,128)(2,1)}), bf16[512,5376]{0,1:T(8,128)(2,1)}) %all-gather.7.cloned.1.call-update) | async-done | bytes 5505040 | tf_op jit(solution)/shard_map/all_gather | solution.py:52
  50.9 3.8 fusion.6
  54.7 99.4 %all-gather.11.cloned.1.call-done = bf16[5376,512]{1,0:T(8,128)(2,1)} async-done(((bf16[1344,512]{1,0:T(8,128)(2,1)}), bf16[5376,512]{1,0:T(8,128)(2,1)}) %all-gather.11.cloned.1.call-update) | async-done | bytes 5505040 | tf_op jit(solution)/shard_map/all_gather | solution.py:60
  154.1 7.6 %multiply_reduce_fusion.2 = (f32[512,4]{0,1:T(4,128)S(1)}, f32[512,512]{0,1:T(8,128)S(1)}) fusion(bf16[5376,512]{1,0:T(8,128)(2,1)} %all-gather.11.cloned.1.call-done, bf16[512,5376]{0,1:T(8,128)(2,1)} %all-gather.7.cloned.1.call-done, f32[5376]{0:T(1024)S(1)} %copy-done.6, f32[512]{0:T(512)S(1)} %add_rsqrt_fusion.3), kind=kOutput, calls=%fused_computation.35 | convolution fusion | flops 2830104576 | bytes 12090368 | tf_op jit(solution)/shard_map/dot_general | solution.py:57
  163.4 1.3 collective-permute-start.2
  164.7 2.4 collective-permute-start.3
  167.0 109.7 %all-gather.9.cloned.1.call-done = bf16[5376,512]{1,0:T(8,128)(2,1)} async-done(((bf16[1344,512]{1,0:T(8,128)(2,1)}), bf16[5376,512]{1,0:T(8,128)(2,1)}) %all-gather.9.cloned.1.call-update) | async-done | bytes 5505040 | tf_op jit(solution)/shard_map/all_gather | solution.py:61
  276.7 7.4 convolution_convert_fusion
  284.1 1.3 collective-permute-start
  285.4 15.4 %collective-permute-start.1 = (bf16[512,512]{1,0:T(8,128)(2,1)S(1)}, bf16[512,512]{1,0:T(8,128)(2,1)}, u32[]{:S(2)}, u32[]{:S(2)}) collective-permute-start(bf16[512,512]{1,0:T(8,128)(2,1)S(1)} %convolution_convert_fusion), channel_id=1, source_target_pairs={{0,4},{4,8},{8,12},{1,5},{5,9},{9,13},{2,6},{6,10},{10,14},{3,7},{... | collective-permute-start | bytes 1572872 | tf_op jit(solution)/shard_map/ppermute | solution.py:17
  300.8 2.0 fusion.12
  302.8 1.0 copy.34
  303.8 1.0 copy.35
  304.8 77.9 %collective-permute-done.1 = bf16[512,512]{1,0:T(8,128)(2,1)} collective-permute-done((bf16[512,512]{1,0:T(8,128)(2,1)S(1)}, bf16[512,512]{1,0:T(8,128)(2,1)}, u32[]{:S(2)}, u32[]{:S(2)}) %collective-permute-start.1) | collective-permute-done | bytes 524320 | tf_op jit(solution)/shard_map/ppermute | solution.py:17
  382.7 1.3 pad_maximum_fusion
  384.0 1.6 copy.45
  385.6 99.2 %all-gather.13.cloned.1.call-done = bf16[5376,1024]{1,0:T(8,128)(2,1)} async-done(((bf16[1344,1024]{1,0:T(8,128)(2,1)}), bf16[5376,1024]{1,0:T(8,128)(2,1)}) %all-gather.13.cloned.1.call-update) | async-done | bytes 11010064 | tf_op jit(solution)/shard_map/all_gather | solution.py:59
  484.8 11.7 %convolution_bitcast_fusion = f32[64,8,8,128]{3,1,2,0:T(8,128)S(1)} fusion(bf16[5376,1024]{1,0:T(8,128)(2,1)} %all-gather.13.cloned.1.call-done, bf16[512,5376]{0,1:T(8,128)(2,1)} %all-gather.7.cloned.1.call-done, f32[5376]{0:T(1024)S(1)} %copy-done.6, f32[512]{0:T(512)S(1)} %add_rsqrt_fusion.3), kind=kOutput, calls=%fused_computation.25 | convolution fusion | flops 5648154624 | bytes 18635776 | tf_op jit(solution)/shard_map/dot_general | solution.py:57
  497.9 1.1 multiply_multiply_fusion
  499.0 0.9 subtract_convert_fusion
  500.2 0.7 copy-done.1
  501.0 13.5 %fusion.14 = f32[4,1536,512,2]{2,1,3,0:T(8,128)} fusion(bf16[512,4,128]{2,0,1:T(8,128)(2,1)S(1)} %maximum_convert_fusion, bf16[512,4,128]{2,0,1:T(8,128)(2,1)S(1)} %copy-done.2, bf16[512,4,128]{2,0,1:T(8,128)(2,1)S(1)} %copy-done.1, bf16[512,4,2,64]{3,0,2,1:T(8,128)(2,1)S(1)} %bitcast.48, bf16[512,4,2,64]{3,0,2,1:T(8,128)(2,1)S(1)} %bitcast.50), kind=kOutput, calls=%fused_computation.36 | convolution fusion | flops 1617428480 | bytes 27787264 | tf_op jit(solution)/shard_map/qhgd,shd->hgqs/dot_general | solution.py:94
  514.5 10.6 %fusion.30 = f32[4,2,512]{2,1,0:T(2,128)S(1)} fusion(pred[512,1536]{0,1:T(8,128)(4,1)} %fusion.12, bf16[512,4,128]{2,0,1:T(8,128)(2,1)S(1)} %maximum_convert_fusion, bf16[512,4,128]{2,0,1:T(8,128)(2,1)} %copy.35, bf16[512,4,128]{2,0,1:T(8,128)(2,1)S(1)} %copy-done.1, bf16[512,4,2,64]{3,0,2,1:T(8,128)(2,1)S(1)} %bitcast.49, ...), kind=kOutput, calls=%fused_computation.56 | convolution fusion | flops 1642595840 | bytes 3424256 | tf_op jit(solution)/shard_map/sub | solution.py:104
  525.2 15.3 %fusion.13 = bf16[4,128,2,512]{3,1,2,0:T(8,128)(2,1)} fusion(bf16[1536,4,128,1]{0,2,3,1:T(8,128)(2,1)} %bitcast.52, f32[4,2,512]{2,1,0:T(2,128)S(1)} %fusion.30, f32[4,1536,512,2]{2,1,3,0:T(8,128)} %fusion.14, pred[512,1536]{0,1:T(8,128)(4,1)} %fusion.12), kind=kOutput, calls=%fused_computation.28 | convolution fusion | flops 1642599936 | bytes 28590080 | tf_op jit(solution)/shard_map/hgqs,shd->qhgd/dot_general | solution.py:106
  540.5 153.9 %all-gather.17.cloned.1.call-done = bf16[4096,1344]{0,1:T(8,128)(2,1)} async-done(((bf16[1024,1344]{0,1:T(8,128)(2,1)}), bf16[4096,1344]{0,1:T(8,128)(2,1)}) %all-gather.17.cloned.1.call-update) | async-done | bytes 11010064 | tf_op jit(solution)/shard_map/all_gather | solution.py:116
  694.4 35.0 %all-gather.15.cloned.1.call-done = bf16[512,4096]{0,1:T(8,128)(2,1)} async-done(((bf16[512,1024]{0,1:T(8,128)(2,1)}), bf16[512,4096]{0,1:T(8,128)(2,1)}) %all-gather.15.cloned.1.call-update) | async-done | bytes 4194320 | tf_op jit(solution)/shard_map/all_gather | solution.py:113
  729.4 10.9 %multiply_reduce_fusion = (f32[512]{0:T(512)S(1)}, f32[512,1344]{0,1:T(8,128)}) fusion(bf16[4096,1344]{0,1:T(8,128)(2,1)} %all-gather.17.cloned.1.call-done, bf16[512,4096]{0,1:T(8,128)(2,1)} %all-gather.15.cloned.1.call-done), kind=kOutput, calls=%fused_computation.20 | convolution fusion | flops 5638520320 | bytes 17958912 | tf_op jit(solution)/shard_map/dot_general | solution.py:114
  740.3 6.9 psum.7
  747.2 3.3 add_convert_fusion
  (46 shorter events, 5.4 us)
Async XLA Ops:
  6.5 44.4 %all-gather.7.cloned.1.call-start = ((), (), s32[]{:S(2)}) async-start(), calls=%async_computation | async-start | bytes 6881280 | tf_op jit(solution)/shard_map/all_gather | solution.py:52
  7.3 146.8 %all-gather.11.cloned.1.call-start = ((), (), s32[]{:S(2)}) async-start(), calls=%async_computation.2 | async-start | bytes 6881280 | tf_op jit(solution)/shard_map/all_gather | solution.py:60
  8.0 268.7 %all-gather.9.cloned.1.call-start = ((), (), s32[]{:S(2)}) async-start(), calls=%async_computation.1 | async-start | bytes 6881280 | tf_op jit(solution)/shard_map/all_gather | solution.py:61
  8.7 476.1 %all-gather.13.cloned.1.call-start = ((), (), s32[]{:S(2)}) async-start(), calls=%async_computation.3 | async-start | bytes 13762560 | tf_op jit(solution)/shard_map/all_gather | solution.py:59
  9.3 685.1 %all-gather.17.cloned.1.call-start = ((), (), s32[]{:S(2)}) async-start(), calls=%async_computation.5 | async-start | bytes 13762560 | tf_op jit(solution)/shard_map/all_gather | solution.py:116
  9.9 144.2 %copy-start.6 = (f32[5376]{0:T(1024)S(1)}, f32[5376]{0:T(1024)}, u32[]{:S(2)}) copy-start(f32[5376]{0:T(1024)} %param.10) | copy-start | bytes 64516
  9.9 719.4 %all-gather.15.cloned.1.call-start = ((), (), s32[]{:S(2)}) async-start(), calls=%async_computation.4 | async-start | bytes 5242880 | tf_op jit(solution)/shard_map/all_gather | solution.py:113
  54.7 107.4 %copy-start.4 = (f32[128]{0:T(128)S(1)}, f32[128]{0:T(128)}, u32[]{:S(2)}) copy-start(f32[128]{0:T(128)} %param.15) | copy-start | bytes 1540
  163.4 139.4 %collective-permute-start.2 = (bf16[512,512]{0,1:T(8,128)(2,1)S(1)}, bf16[512,512]{0,1:T(8,128)(2,1)S(1)}, u32[]{:S(2)}, u32[]{:S(2)}) collective-permute-start(bf16[512,512]{0,1:T(8,128)(2,1)S(1)} %bitcast.55), channel_id=1, source_target_pairs={{0,8},{4,12},{1,9},{5,13},{2,10},{6,14},{3,11},{7,15},{16,24},{20,... | collective-permute-start | bytes 1572872 | tf_op jit(solution)/shard_map/ppermute | solution.py:17
  164.7 139.1 %collective-permute-start.3 = (bf16[512,512]{0,1:T(8,128)(2,1)S(1)}, bf16[512,512]{0,1:T(8,128)(2,1)S(1)}, u32[]{:S(2)}, u32[]{:S(2)}) collective-permute-start(bf16[512,512]{0,1:T(8,128)(2,1)S(1)} %bitcast.56), channel_id=1, source_target_pairs={{0,4},{4,8},{8,12},{1,5},{5,9},{9,13},{2,6},{6,10},{10,14},{3,7},{... | collective-permute-start | bytes 1572872 | tf_op jit(solution)/shard_map/ppermute | solution.py:17
  284.1 20.7 %collective-permute-start = (bf16[512,512]{1,0:T(8,128)(2,1)S(1)}, bf16[512,512]{1,0:T(8,128)(2,1)}, u32[]{:S(2)}, u32[]{:S(2)}) collective-permute-start(bf16[512,512]{1,0:T(8,128)(2,1)S(1)} %convolution_convert_fusion), channel_id=1, source_target_pairs={{0,8},{4,12},{1,9},{5,13},{2,10},{6,14},{3,11},{7,15},{16,24},{20,... | collective-permute-start | bytes 1572872 | tf_op jit(solution)/shard_map/ppermute | solution.py:17
  285.4 97.3 %collective-permute-start.1 = (bf16[512,512]{1,0:T(8,128)(2,1)S(1)}, bf16[512,512]{1,0:T(8,128)(2,1)}, u32[]{:S(2)}, u32[]{:S(2)}) collective-permute-start(bf16[512,512]{1,0:T(8,128)(2,1)S(1)} %convolution_convert_fusion), channel_id=1, source_target_pairs={{0,4},{4,8},{8,12},{1,5},{5,9},{9,13},{2,6},{6,10},{10,14},{3,7},{... | collective-permute-start | bytes 1572872 | tf_op jit(solution)/shard_map/ppermute | solution.py:17
  496.5 1.4 copy-start.5
  499.8 1.0 copy-start.1
  499.9 1.2 copy-start.2
  540.5 206.7 %copy-start = (bf16[512,1344]{0,1:T(8,128)(2,1)S(1)}, bf16[512,1344]{0,1:T(8,128)(2,1)}, u32[]{:S(2)}) copy-start(bf16[512,1344]{0,1:T(8,128)(2,1)} %param.9) | copy-start | bytes 4128772
  540.5 206.7 %copy-start.3 = (f32[1344]{0:T(1024)S(1)}, f32[1344]{0:T(1024)}, u32[]{:S(2)}) copy-start(f32[1344]{0:T(1024)} %param.17) | copy-start | bytes 16132
Sparse Core Ops, SparseCore 0:
  8.9 41.9 all-gather.6
  52.5 101.5 all-gather.10
  155.7 121.0 all-gather.8
  278.1 206.6 all-gather.12
  486.2 208.1 all-gather.16
  695.8 33.5 all-gather.14
where the time goes:
time: 759 us; the launch traced here: 757 us
  waiting for transfers between devices  618 us (81%)
  matrix products  77.1 us (10%)
  starting transfers between devices  20.5 us (3%)
  other arithmetic  15.1 us (2%)
  between operations  13.8 us (2%)
    all_gather x1, waiting for transfers between devices, on_device(): lax.all_gather(output_weight, 'row', axis=0, tiled=True)  154 us
    all_gather x1, waiting for transfers between devices, on_device(): lax.all_gather(value_matrix, 'row', axis=0, tiled=True)  110 us
    all_gather x1, waiting for transfers between devices, on_device(): lax.all_gather(key_matrix, 'row', axis=0, tiled=True)  99.4 us
    all_gather x1, waiting for transfers between devices, on_device(): lax.all_gather(query_weight, 'row', axis=0, tiled=True)  99.2 us
    ppermute x4, waiting for transfers between devices, shifted(): return lax.ppermute(x, axis, pairs)  77.9 us
    all_gather x1, waiting for transfers between devices, on_device(): token_rows = lax.all_gather(stream_in, ('col', 'sub'), axis=1, tiled=True)  39.9 us
    all_gather x1, waiting for transfers between devices, on_device(): head_rows = lax.all_gather(heads_out, ('col', 'sub'), axis=1, tiled=True)  35 us
    dot_general x3, matrix products, add_panel(): return jnp.dot(normed, panel_piece, preferred_element_type=jnp.float32)  26.7 us
  transfers between devices with their start and end apart: 10, of which 7 were waited for; matrix products, arithmetic and copies ran while one was open for 11% of the time, Pallas kernels for 0%

commit v1 on v0

--- a/solution.py
+++ b/solution.py
@@ -121,6 +121,143 @@
     return (stream_in.astype(jnp.float32) + scaled).astype(jnp.bfloat16)
 
 
+def swapped(x):
+    count = lax.axis_size("groups")
+    return lax.ppermute(x, "groups", [(i, count - 1 - i) for i in range(count)])
+
+
+def rows_gathered(piece):
+    return lax.all_gather(piece, "row", axis=0)
+
+
+def attend(query_rot, keys_flat, values_flat, row_index, head_size, scale_factor):
+    tokens, kv_width = keys_flat.shape
+    pair_heads = kv_width // head_size
+    group_count = query_rot.shape[1] // pair_heads
+    query_places = row_index * tokens + jnp.arange(tokens, dtype=jnp.int32)
+    shards_back = min(WINDOW_LENGTH // tokens, lax.axis_size("row") - 1)
+    band_length = (shards_back + 1) * tokens
+    key_parts = [keys_flat]
+    value_parts = [values_flat]
+    for offset in range(1, shards_back + 1):
+        keys_prior, values_prior = shifted((keys_flat, values_flat), "row", offset)
+        key_parts = [keys_prior] + key_parts
+        value_parts = [values_prior] + value_parts
+    keys_band = jnp.concatenate(key_parts, axis=0)
+    values_band = jnp.concatenate(value_parts, axis=0)
+    key_places = (row_index - shards_back) * tokens + jnp.arange(band_length, dtype=jnp.int32)
+    distance = query_places[:, None] - key_places[None, :]
+    visible = (distance >= 0) & (distance < WINDOW_LENGTH) & (key_places[None, :] >= 0)
+    grouped = query_rot.reshape(tokens, pair_heads, group_count, head_size)
+    scores = (
+        jnp.einsum(
+            "qhgd,shd->hgqs",
+            grouped,
+            keys_band.reshape(band_length, pair_heads, head_size),
+            preferred_element_type=jnp.float32,
+        )
+        * scale_factor
+    )
+    scores = jnp.where(visible, scores, -1e30)
+    row_max = jnp.max(scores, axis=-1, keepdims=True)
+    exponent = jnp.exp(scores - row_max)
+    weights = (exponent / jnp.sum(exponent, axis=-1, keepdims=True)).astype(jnp.bfloat16)
+    attended = jnp.einsum(
+        "hgqs,shd->qhgd",
+        weights,
+        values_band.reshape(band_length, pair_heads, head_size),
+        preferred_element_type=jnp.float32,
+    )
+    return attended.reshape(tokens, -1).astype(jnp.bfloat16)
+
+
+def on_device_sharing(
+    stream_in,
+    in_gain,
+    query_weight,
+    key_matrix,
+    value_matrix,
+    query_gain,
+    key_norm_gain,
+    output_weight,
+    post_gain,
+):
+    group = lax.axis_index("groups")
+    head_size = query_gain.shape[0]
+    rows = lax.axis_size("row")
+
+    def own_columns(w):
+        width = w.shape[1] // 2
+        return lax.dynamic_slice_in_dim(w, group * width, width, axis=1)
+
+    def halves(w):
+        own = rows_gathered(own_columns(w))
+        other = swapped(own)
+        full = rows * w.shape[0]
+        return own.reshape(full, -1), other.reshape(full, -1)
+
+    key_halves = halves(key_matrix)
+    token_rows = lax.all_gather(stream_in, ("col", "sub"), axis=1, tiled=True)
+    value_halves = halves(value_matrix)
+    query_halves = halves(query_weight)
+    depth = output_weight.shape[0]
+    half, quarter = depth // 2, depth // 4
+    out_own = rows_gathered(lax.dynamic_slice_in_dim(output_weight, group * half, half, axis=0))
+    out_peer = swapped(out_own[:, :quarter])
+    out_direct = rows_gathered(
+        lax.dynamic_slice_in_dim(output_weight, (1 - group) * half + quarter, quarter, axis=0)
+    )
+
+    tokens = token_rows.shape[0]
+    normed = root_mean_scale(token_rows.astype(jnp.float32), in_gain).astype(jnp.bfloat16)
+
+    def add_panel(panel):
+        return jnp.dot(normed, panel, preferred_element_type=jnp.float32)
+
+    scale_factor = float(MODEL_WIDTH // QUERY_HEAD_COUNT) ** (-0.5)
+    row_index = lax.axis_index("row")
+    places = (row_index * tokens + jnp.arange(tokens, dtype=jnp.int32)).astype(jnp.float32)
+
+    def rotated(projected, gain):
+        heads = projected.reshape(tokens, -1, head_size)
+        return apply_rotary(root_mean_scale(heads, gain), places).astype(jnp.bfloat16)
+
+    attended = []
+    for i in range(2):
+        keys_flat = rotated(add_panel(key_halves[i]), key_norm_gain).reshape(tokens, -1)
+        values_flat = add_panel(value_halves[i]).astype(jnp.bfloat16)
+        query_rot = rotated(add_panel(query_halves[i]), query_gain)
+        heads_out = attend(query_rot, keys_flat, values_flat, row_index, head_size, scale_factor)
+        attended.append(lax.all_gather(heads_out, ("col", "sub"), axis=1, tiled=True))
+    own_rows, other_rows = attended
+    blocks = other_rows.reshape(tokens, -1, half)
+    branch = (
+        jnp.dot(own_rows, out_own.reshape(-1, out_own.shape[-1]), preferred_element_type=jnp.float32)
+        + jnp.dot(
+            blocks[:, :, quarter:].reshape(tokens, -1),
+            out_direct.reshape(-1, out_direct.shape[-1]),
+            preferred_element_type=jnp.float32,
+        )
+        + jnp.dot(
+            blocks[:, :, :quarter].reshape(tokens, -1),
+            out_peer.reshape(-1, out_peer.shape[-1]),
+            preferred_element_type=jnp.float32,
+        )
+    )
+    squares = lax.psum(jnp.sum(branch * branch, axis=-1), ("col", "sub"))
+    scaled = branch * lax.rsqrt(squares[:, None] / MODEL_WIDTH + EPSILON) * post_gain
+    return (stream_in.astype(jnp.float32) + scaled).astype(jnp.bfloat16)
+
+
+def on_device_any(*operands):
+    head_size = operands[5].shape[0]
+    pair_heads = operands[3].shape[1] // head_size
+    blocks_agree = lax.axis_size("row") == lax.axis_size("col") * lax.axis_size("sub")
+    if lax.axis_size("groups") == 2 and pair_heads % 2 == 0 and blocks_agree:
+        return on_device_sharing(*operands)
+    return on_device(*operands)
+
+
 def solution(mesh):
     placed = (
         P(("groups", "row"), ("col", "sub")),
@@ -134,7 +271,7 @@
         P(("col", "sub")),
     )
     return jax.shard_map(
-        on_device,
+        on_device_any,
         mesh=mesh,
         in_specs=placed,
         out_specs=P(("groups", "row"), ("col", "sub")),

time: 759 us -> 618 us (0.81)
  waiting for transfers between devices: 618 us -> 417 us
  local copies, waits for them, and re-layouts: 6.05 us -> 55.9 us
    all_gather x6 -> x8, waiting for transfers between devices: 537 us -> 239 us  [the longest x5 202 us: rows_gathered(): return lax.all_gather(piece, 'row', axis=0)]
    ppermute x0 -> x4, waiting for transfers between devices: none -> 107 us  [swapped(): return lax.ppermute(x, 'groups', [(i, count - 1 - i) for i in range(count)])]
    dot_general x0 -> x4, local copies, waits for them, and re-layouts: none -> 24.2 us  [add_panel(): return jnp.dot(normed, panel, preferred_element_type=jnp.float32)]
    all_gather x0 -> x2, local copies, waits for them, and re-layouts: none -> 13.2 us  [rows_gathered(): return lax.all_gather(piece, 'row', axis=0)]
    sub x1 -> x2, matrix products: 10.6 us -> 21.7 us  [attend(): exponent = jnp.exp(scores - row_max)]
    dynamic_slice x0 -> x5, local copies, waits for them, and re-layouts: none -> 8.92 us  [the longest x3 6.66 us: own_columns(): return lax.dynamic_slice_in_dim(w, group * width, width, axis=1)]
    ppermute x4 -> x8, waiting for transfers between devices: 77.9 us -> 70.4 us  [shifted(): return lax.ppermute(x, axis, pairs)]
    ppermute x4 -> x8, starting transfers between devices: 20.3 us -> 15.2 us  [shifted(): return lax.ppermute(x, axis, pairs)]
  transfers between devices with their start and end apart: 10 -> 20, of which waited for: 7 -> 10; matrix products, arithmetic and copies ran while one was open for 11% -> 23% of each run, Pallas kernels for 0% -> 0%
where the time goes in v1:
time: 618 us; the launch traced here: 609 us
  waiting for transfers between devices  417 us (67%)
  matrix products  84.1 us (14%)
  local copies, waits for them, and re-layouts  55.9 us (9%)
  starting transfers between devices  18 us (3%)
  between operations  14.3 us (2%)
  other arithmetic  13.6 us (2%)
    all_gather x5, waiting for transfers between devices, rows_gathered(): return lax.all_gather(piece, 'row', axis=0)  202 us
    ppermute x4, waiting for transfers between devices, swapped(): return lax.ppermute(x, 'groups', [(i, count - 1 - i) for i in range(count)])  107 us
    ppermute x8, waiting for transfers between devices, shifted(): return lax.ppermute(x, axis, pairs)  70.4 us
    all_gather x1, waiting for transfers between devices, on_device_sharing(): token_rows = lax.all_gather(stream_in, ('col', 'sub'), axis=1, tiled=True)  37.3 us
    dot_general x6, matrix products, add_panel(): return jnp.dot(normed, panel, preferred_element_type=jnp.float32)  31.8 us
    dot_general x4, local copies, waits for them, and re-layouts, add_panel(): return jnp.dot(normed, panel, preferred_element_type=jnp.float32)  24.2 us
    sub x2, matrix products, attend(): exponent = jnp.exp(scores - row_max)  21.7 us
    ppermute x8, starting transfers between devices, shifted(): return lax.ppermute(x, axis, pairs)  15.2 us
  transfers between devices with their start and end apart: 20, of which 10 were waited for; matrix products, arithmetic and copies ran while one was open for 23% of the time, Pallas kernels for 0%

profile of v1, /device:TPU:22, one launch (start us, length us, event | category | flops | bytes accessed | tf_op | source)
XLA Modules:
  0.0 609.0 jit_solution(1578314653373979051)
XLA Ops:
  15.3 50.3 %all-gather.22.cloned.1.call-done = bf16[5376,256]{1,0:T(8,128)(2,1)} async-done(((bf16[1344,256]{1,0:T(8,128)(2,1)}), bf16[5376,256]{1,0:T(8,128)(2,1)}) %all-gather.22.cloned.1.call-update) | async-done | bytes 2752528 | tf_op jit(solution)/shard_map/all_gather | solution.py:130
  67.8 100.0 %all-gather.24.cloned.1.call-done = bf16[5376,512]{1,0:T(8,128)(2,1)} async-done(((bf16[1344,512]{1,0:T(8,128)(2,1)}), bf16[5376,512]{1,0:T(8,128)(2,1)}) %all-gather.24.cloned.1.call-update) | async-done | bytes 5505040 | tf_op jit(solution)/shard_map/all_gather | solution.py:130
  173.6 51.5 %all-gather.20.cloned.1.call-done = bf16[5376,256]{1,0:T(8,128)(2,1)} async-done(((bf16[1344,256]{1,0:T(8,128)(2,1)}), bf16[5376,256]{1,0:T(8,128)(2,1)}) %all-gather.20.cloned.1.call-update) | async-done | bytes 2752528 | tf_op jit(solution)/shard_map/all_gather | solution.py:130
  225.7 4.6 copy.37
  230.3 37.3 %all-gather.14.cloned.1.call-done = bf16[512,5376]{0,1:T(8,128)(2,1)} async-done(((bf16[512,1344]{0,1:T(8,128)(2,1)}), bf16[512,5376]{0,1:T(8,128)(2,1)}) %all-gather.14.cloned.1.call-update) | async-done | bytes 5505040 | tf_op jit(solution)/shard_map/all_gather | solution.py:200
  267.5 3.9 fusion.2
  271.7 3.7 multiply_reduce_fusion.3
  280.4 3.4 collective-permute-start.9
  283.8 63.6 %collective-permute-done.4 = bf16[4,1344,256]{2,1,0:T(8,128)(2,1)} collective-permute-done((bf16[4,1344,256]{2,1,0:T(8,128)(2,1)}, bf16[4,1344,256]{2,1,0:T(8,128)(2,1)}, u32[]{:S(2)}, u32[]{:S(2)}) %collective-permute-start.4) | collective-permute-done | bytes 2752544 | tf_op jit(solution)/shard_map/ppermute | solution.py:126
  347.4 4.5 convolution_convert_fusion
  356.0 8.2 %copy.30 = bf16[512,5376]{1,0:T(8,128)(2,1)} copy(bf16[512,5376]{0,1:T(8,128)(2,1)} %bitcast.135) | data formatting | bytes 11010048 | tf_op jit(solution)/shard_map/dot_general | solution.py:215
  364.3 8.3 %multiply_reduce_fusion.2 = (f32[512,4]{0,1:T(4,128)S(1)}, f32[512,4,128]{0,2,1:T(8,128)}) fusion(bf16[4,128,5376]{2,1,0:T(8,128)(2,1)} %bitcast.137, f32[5376]{0:T(1024)S(1)} %copy-done.11, f32[512]{0:T(512)S(1)} %add_rsqrt_fusion.5, bf16[512,5376]{0,1:T(8,128)(2,1)} %all-gather.14.cloned.1.call-done), kind=kOutput, calls=%fused_computation.52 | convolution fusion | flops 2830104576 | bytes 12090368 | tf_op jit(solution)/shard_map/dot_general | solution.py:215
  372.6 23.2 %collective-permute-done.6 = bf16[512,256]{1,0:T(8,128)(2,1)S(1)} collective-permute-done((bf16[512,256]{1,0:T(8,128)(2,1)S(1)}, bf16[512,256]{1,0:T(8,128)(2,1)S(1)}, u32[]{:S(2)}, u32[]{:S(2)}) %collective-permute-start.6) | collective-permute-done | bytes 262176 | tf_op jit(solution)/shard_map/ppermute | solution.py:17
  397.1 8.1 %copy.39 = bf16[512,5376]{1,0:T(8,128)(2,1)} copy(bf16[512,5376]{0,1:T(8,128)(2,1)} %bitcast.35) | data formatting | bytes 11010048 | tf_op jit(solution)/shard_map/dot_general | solution.py:215
  405.1 7.4 %multiply_reduce_fusion.1 = (f32[512,4]{0,1:T(4,128)S(1)}, f32[512,4,128]{0,2,1:T(8,128)S(1)}) fusion(bf16[4,128,5376]{2,1,0:T(8,128)(2,1)} %bitcast.136, f32[5376]{0:T(1024)S(1)} %copy-done.11, f32[512]{0:T(512)S(1)} %add_rsqrt_fusion.5, bf16[512,5376]{0,1:T(8,128)(2,1)} %all-gather.14.cloned.1.call-done), kind=kOutput, calls=%fused_computation.50 | convolution fusion | flops 2830104576 | bytes 12090368 | tf_op jit(solution)/shard_map/dot_general | solution.py:215
  414.0 11.0 %fusion.55 = (f32[2,2,512]{2,1,0:T(2,128)S(1)}, f32[2,2,512,1536]{2,3,1,0:T(8,128)}) fusion(pred[512,1536]{0,1:T(8,128)(4,1)} %fusion.25, bf16[512,2,128]{0,2,1:T(8,128)(2,1)} %maximum_convert_fusion.1, bf16[512,2,128]{0,2,1:T(8,128)(2,1)} %bitcast.30, bf16[512,2,128]{0,2,1:T(8,128)(2,1)} %bitcast.29, bf16[512,2,2,64]{3,0,2,1:T(8,128)(2,1)S(1)} %copy.42, ...), kind=kOutput, calls=%fused_computation.101 | convolution fusion | flops 821298688 | bytes 14688256 | tf_op jit(solution)/shard_map/sub | solution.py:163
  425.0 6.4 %fusion.30 = bf16[2,128,2,512]{3,1,2,0:T(8,128)(2,1)} fusion(bf16[1536,2,128,1]{0,2,3,1:T(8,128)(2,1)S(1)} %bitcast.147, f32[2,2,512,1536]{2,3,1,0:T(8,128)} %get-tuple-element.32, f32[2,2,512]{2,1,0:T(2,128)S(1)} %get-tuple-element.31), kind=kOutput, calls=%fused_computation.43 | convolution fusion | flops 811859968 | bytes 13901824 | tf_op jit(solution)/shard_map/hgqs,shd->qhgd/dot_general | solution.py:165
  431.8 6.0 convolution_convert_fusion.1
  444.9 10.4 %collective-permute-done = bf16[512,256]{1,0:T(8,128)(2,1)S(1)} collective-permute-done((bf16[512,256]{1,0:T(8,128)(2,1)S(1)}, bf16[512,256]{1,0:T(8,128)(2,1)S(1)}, u32[]{:S(2)}, u32[]{:S(2)}) %collective-permute-start) | collective-permute-done | bytes 262176 | tf_op jit(solution)/shard_map/ppermute | solution.py:17
  455.3 25.9 %collective-permute-done.1 = bf16[512,256]{1,0:T(8,128)(2,1)S(1)} collective-permute-done((bf16[512,256]{1,0:T(8,128)(2,1)S(1)}, bf16[512,256]{1,0:T(8,128)(2,1)S(1)}, u32[]{:S(2)}, u32[]{:S(2)}) %collective-permute-start.1) | collective-permute-done | bytes 262176 | tf_op jit(solution)/shard_map/ppermute | solution.py:17
  482.2 10.8 %collective-permute-done.3 = bf16[512,256]{0,1:T(8,128)(2,1)} collective-permute-done((bf16[512,256]{0,1:T(8,128)(2,1)}, bf16[512,256]{0,1:T(8,128)(2,1)}, u32[]{:S(2)}, u32[]{:S(2)}) %collective-permute-start.3) | collective-permute-done | bytes 262176 | tf_op jit(solution)/shard_map/ppermute | solution.py:17
  493.0 10.7 %fusion.56 = (f32[2,2,512]{2,1,0:T(2,128)S(1)}, f32[2,2,512,1536]{2,3,1,0:T(8,128)}) fusion(pred[512,1536]{0,1:T(8,128)(4,1)S(1)} %copy-done.4, bf16[512,2,128]{0,2,1:T(8,128)(2,1)} %maximum_convert_fusion, bf16[512,2,128]{0,2,1:T(8,128)(2,1)} %bitcast.8, bf16[512,2,128]{0,2,1:T(8,128)(2,1)} %bitcast.7, bf16[512,2,2,64]{3,0,2,1:T(8,128)(2,1)S(1)} %copy.33, ...), kind=kOutput, calls=%fused_computation.102 | convolution fusion | flops 821298688 | bytes 14688256 | tf_op jit(solution)/shard_map/sub | solution.py:163
  503.7 6.4 %fusion.31 = bf16[2,128,2,512]{3,1,2,0:T(8,128)(2,1)} fusion(bf16[1536,2,128,1]{0,2,3,1:T(8,128)(2,1)S(1)} %bitcast.148, f32[2,2,512,1536]{2,3,1,0:T(8,128)} %get-tuple-element.34, f32[2,2,512]{2,1,0:T(2,128)S(1)} %get-tuple-element.33), kind=kOutput, calls=%fused_computation.44 | convolution fusion | flops 811859968 | bytes 13901824 | tf_op jit(solution)/shard_map/hgqs,shd->qhgd/dot_general | solution.py:165
  510.2 8.6 %copy.50 = bf16[2048,1344]{1,0:T(8,128)(2,1)} copy(bf16[2048,1344]{0,1:T(8,128)(2,1)} %all-gather.26.cloned.1.call-done) | data formatting | bytes 11010048 | tf_op jit(solution)/shard_map/all_gather | solution.py:130
  518.8 3.7 slice.53
  526.1 4.5 copy.47
  530.7 5.4 convolution_bitcast_fusion.1
  536.1 7.3 %convolution_add_fusion = f32[512,1344]{0,1:T(8,128)S(1)} fusion(f32[512,1344]{0,1:T(8,128)} %convolution_bitcast_fusion.1, bf16[2048,1344]{0,1:T(8,128)(2,1)} %all-gather.26.cloned.1.call-done, bf16[512,2048]{0,1:T(8,128)(2,1)} %all-gather.16.cloned.1.call-done), kind=kOutput, calls=%fused_computation.33 | convolution fusion | flops 2819260416 | bytes 13107200 | tf_op jit(solution)/shard_map/dot_general | solution.py:235
  543.4 43.6 %collective-permute-done.11 = bf16[4,256,1344]{1,2,0:T(8,128)(2,1)} collective-permute-done((bf16[4,256,1344]{1,2,0:T(8,128)(2,1)S(1)}, bf16[4,256,1344]{1,2,0:T(8,128)(2,1)}, u32[]{:S(2)}, u32[]{:S(2)}) %collective-permute-start.11) | collective-permute-done | bytes 2752544 | tf_op jit(solution)/shard_map/ppermute | solution.py:126
  587.0 5.2 multiply_reduce_fusion
  592.1 5.9 psum.7
  598.0 3.7 add_convert_fusion
  (96 shorter events, 41.3 us)
Async XLA Ops:
  6.5 7.5 %copy-start = (bf16[1024,1344]{0,1:T(8,128)(2,1)S(1)}, bf16[1024,1344]{0,1:T(8,128)(2,1)}, u32[]{:S(2)}) copy-start(bf16[1024,1344]{0,1:T(8,128)(2,1)} %param.16) | copy-start | bytes 8257540
  6.5 59.1 %all-gather.22.cloned.1.call-start = ((), (), s32[]{:S(2)}) async-start(), calls=%async_computation.4 | async-start | bytes 3440640 | tf_op jit(solution)/shard_map/all_gather | solution.py:130
  8.7 159.1 %all-gather.24.cloned.1.call-start = ((), (), s32[]{:S(2)}) async-start(), calls=%async_computation.5 | async-start | bytes 6881280 | tf_op jit(solution)/shard_map/all_gather | solution.py:130
  11.3 213.8 %all-gather.20.cloned.1.call-start = ((), (), s32[]{:S(2)}) async-start(), calls=%async_computation.3 | async-start | bytes 3440640 | tf_op jit(solution)/shard_map/all_gather | solution.py:130
  13.4 254.2 %all-gather.14.cloned.1.call-start = ((), (), s32[]{:S(2)}) async-start(), calls=%async_computation | async-start | bytes 6881280 | tf_op jit(solution)/shard_map/all_gather | solution.py:200
  14.0 496.2 %all-gather.26.cloned.1.call-start = ((), (), s32[]{:S(2)}) async-start(), calls=%async_computation.6 | async-start | bytes 6881280 | tf_op jit(solution)/shard_map/all_gather | solution.py:130
  15.3 510.9 %all-gather.28.cloned.1.call-start = ((), (), s32[]{:S(2)}) async-start(), calls=%async_computation.7 | async-start | bytes 3440640 | tf_op jit(solution)/shard_map/all_gather | solution.py:130
  65.6 160.1 %collective-permute-start.7 = (bf16[4,1344,256]{2,1,0:T(8,128)(2,1)}, bf16[4,1344,256]{2,1,0:T(8,128)(2,1)}, u32[]{:S(2)}, u32[]{:S(2)}) collective-permute-start(bf16[4,1344,256]{2,1,0:T(8,128)(2,1)} %bitcast.139), channel_id=1, source_target_pairs={{0,16},{16,0},{1,17},{17,1},{2,18},{18,2},{3,19},{19,3},{4,20},{20... | collective-permute-start | bytes 8257544 | tf_op jit(solution)/shard_map/ppermute | solution.py:126
  67.2 463.5 %all-gather.18.cloned.1.call-start = ((), (), s32[]{:S(2)}) async-start(), calls=%async_computation.2 | async-start | bytes 2621440 | tf_op jit(solution)/shard_map/all_gather | solution.py:231
  167.9 229.2 %collective-permute-start.10 = (bf16[4,1344,512]{2,1,0:T(8,128)(2,1)}, bf16[4,1344,512]{2,1,0:T(8,128)(2,1)}, u32[]{:S(2)}, u32[]{:S(2)}) collective-permute-start(bf16[4,1344,512]{2,1,0:T(8,128)(2,1)} %bitcast.134), channel_id=1, source_target_pairs={{0,16},{16,0},{1,17},{17,1},{2,18},{18,2},{3,19},{19,3},{4,20},{20... | collective-permute-start | bytes 16515080 | tf_op jit(solution)/shard_map/ppermute | solution.py:126
  225.1 122.3 %collective-permute-start.4 = (bf16[4,1344,256]{2,1,0:T(8,128)(2,1)}, bf16[4,1344,256]{2,1,0:T(8,128)(2,1)}, u32[]{:S(2)}, u32[]{:S(2)}) collective-permute-start(bf16[4,1344,256]{2,1,0:T(8,128)(2,1)} %bitcast.151), channel_id=1, source_target_pairs={{0,16},{16,0},{1,17},{17,1},{2,18},{18,2},{3,19},{19,3},{4,20},{20... | collective-permute-start | bytes 8257544 | tf_op jit(solution)/shard_map/ppermute | solution.py:126
  225.7 45.8 %copy-start.11 = (f32[5376]{0:T(1024)S(1)}, f32[5376]{0:T(1024)}, u32[]{:S(2)}) copy-start(f32[5376]{0:T(1024)} %param.10) | copy-start | bytes 64516
  267.5 4.2 copy-start.2
  279.1 134.9 %collective-permute-start.8 = (bf16[512,256]{0,1:T(8,128)(2,1)}, bf16[512,256]{0,1:T(8,128)(2,1)}, u32[]{:S(2)}, u32[]{:S(2)}) collective-permute-start(bf16[512,256]{0,1:T(8,128)(2,1)} %bitcast.28), channel_id=1, source_target_pairs={{0,8},{4,12},{1,9},{5,13},{2,10},{6,14},{3,11},{7,15},{16,24},{20,... | collective-permute-start | bytes 786440 | tf_op jit(solution)/shard_map/ppermute | solution.py:17
  280.4 133.6 %collective-permute-start.9 = (bf16[512,256]{0,1:T(8,128)(2,1)}, bf16[512,256]{0,1:T(8,128)(2,1)}, u32[]{:S(2)}, u32[]{:S(2)}) collective-permute-start(bf16[512,256]{0,1:T(8,128)(2,1)} %bitcast.28), channel_id=1, source_target_pairs={{0,4},{4,8},{8,12},{1,5},{5,9},{9,13},{2,6},{6,10},{10,14},{3,7},{... | collective-permute-start | bytes 786440 | tf_op jit(solution)/shard_map/ppermute | solution.py:17
  351.9 20.7 %collective-permute-start.5 = (bf16[512,256]{1,0:T(8,128)(2,1)S(1)}, bf16[512,256]{1,0:T(8,128)(2,1)S(1)}, u32[]{:S(2)}, u32[]{:S(2)}) collective-permute-start(bf16[512,256]{1,0:T(8,128)(2,1)S(1)} %convolution_convert_fusion), channel_id=1, source_target_pairs={{0,8},{4,12},{1,9},{5,13},{2,10},{6,14},{3,11},{7,15},{16,24},{20,... | collective-permute-start | bytes 786440 | tf_op jit(solution)/shard_map/ppermute | solution.py:17
  353.2 42.6 %collective-permute-start.6 = (bf16[512,256]{1,0:T(8,128)(2,1)S(1)}, bf16[512,256]{1,0:T(8,128)(2,1)S(1)}, u32[]{:S(2)}, u32[]{:S(2)}) collective-permute-start(bf16[512,256]{1,0:T(8,128)(2,1)S(1)} %convolution_convert_fusion), channel_id=1, source_target_pairs={{0,4},{4,8},{8,12},{1,5},{5,9},{9,13},{2,6},{6,10},{10,14},{3,7},{... | collective-permute-start | bytes 786440 | tf_op jit(solution)/shard_map/ppermute | solution.py:17
  405.1 7.4 %copy-start.3 = (f32[512,4,128]{0,2,1:T(8,128)S(1)}, f32[512,4,128]{0,2,1:T(8,128)}, u32[]{:S(2)}) copy-start(f32[512,4,128]{0,2,1:T(8,128)} %get-tuple-element.28) | copy-start | bytes 3145732
  405.1 7.4 %copy-start.9 = (f32[128]{0:T(128)S(1)}, f32[128]{0:T(128)}, u32[]{:S(2)}) copy-start(f32[128]{0:T(128)} %param.14) | copy-start | bytes 1540
  414.0 11.0 %copy-start.5 = (bf16[1536,256]{0,1:T(8,128)(2,1)S(1)}, bf16[1536,256]{0,1:T(8,128)(2,1)}, u32[]{:S(2)}) copy-start(bf16[1536,256]{0,1:T(8,128)(2,1)} %copy.68) | copy-start | bytes 2359300
  425.0 6.7 %copy-start.12 = (f32[5376]{0:T(1024)S(1)}, f32[5376]{0:T(1024)}, u32[]{:S(2)}) copy-start(f32[5376]{0:T(1024)} %param.10) | copy-start | bytes 64516
  431.5 9.5 %copy-start.6 = (bf16[512,2,64]{0,2,1:T(8,128)(2,1)S(1)}, bf16[512,2,64]{0,2,1:T(8,128)(2,1)}, u32[]{:S(2)}) copy-start(bf16[512,2,64]{0,2,1:T(8,128)(2,1)} %get-tuple-element.10) | copy-start | bytes 393220
  431.5 61.5 %copy-start.4 = (pred[512,1536]{0,1:T(8,128)(4,1)S(1)}, pred[512,1536]{0,1:T(8,128)(4,1)}, u32[]{:S(2)}) copy-start(pred[512,1536]{0,1:T(8,128)(4,1)} %fusion.25) | copy-start | bytes 2359300
  431.5 104.6 %all-gather.16.cloned.1.call-start = ((), (), s32[]{:S(2)}) async-start(), calls=%async_computation.1 | async-start | bytes 2621440 | tf_op jit(solution)/shard_map/all_gather | solution.py:231
  437.7 17.6 %collective-permute-start = (bf16[512,256]{1,0:T(8,128)(2,1)S(1)}, bf16[512,256]{1,0:T(8,128)(2,1)S(1)}, u32[]{:S(2)}, u32[]{:S(2)}) collective-permute-start(bf16[512,256]{1,0:T(8,128)(2,1)S(1)} %convolution_convert_fusion.1), channel_id=1, source_target_pairs={{0,8},{4,12},{1,9},{5,13},{2,10},{6,14},{3,11},{7,15},{16,24},{20,... | collective-permute-start | bytes 786440 | tf_op jit(solution)/shard_map/ppermute | solution.py:17
  439.0 42.2 %collective-permute-start.1 = (bf16[512,256]{1,0:T(8,128)(2,1)S(1)}, bf16[512,256]{1,0:T(8,128)(2,1)S(1)}, u32[]{:S(2)}, u32[]{:S(2)}) collective-permute-start(bf16[512,256]{1,0:T(8,128)(2,1)S(1)} %convolution_convert_fusion.1), channel_id=1, source_target_pairs={{0,4},{4,8},{8,12},{1,5},{5,9},{9,13},{2,6},{6,10},{10,14},{3,7},{... | collective-permute-start | bytes 786440 | tf_op jit(solution)/shard_map/ppermute | solution.py:17
  441.7 40.5 %collective-permute-start.2 = (bf16[512,256]{0,1:T(8,128)(2,1)}, bf16[512,256]{0,1:T(8,128)(2,1)}, u32[]{:S(2)}, u32[]{:S(2)}) collective-permute-start(bf16[512,256]{0,1:T(8,128)(2,1)} %bitcast.6), channel_id=1, source_target_pairs={{0,8},{4,12},{1,9},{5,13},{2,10},{6,14},{3,11},{7,15},{16,24},{20,... | collective-permute-start | bytes 786440 | tf_op jit(solution)/shard_map/ppermute | solution.py:17
  443.0 50.0 %collective-permute-start.3 = (bf16[512,256]{0,1:T(8,128)(2,1)}, bf16[512,256]{0,1:T(8,128)(2,1)}, u32[]{:S(2)}, u32[]{:S(2)}) collective-permute-start(bf16[512,256]{0,1:T(8,128)(2,1)} %bitcast.6), channel_id=1, source_target_pairs={{0,4},{4,8},{8,12},{1,5},{5,9},{9,13},{2,6},{6,10},{10,14},{3,7},{... | collective-permute-start | bytes 786440 | tf_op jit(solution)/shard_map/ppermute | solution.py:17
  525.5 61.4 %collective-permute-start.11 = (bf16[4,256,1344]{1,2,0:T(8,128)(2,1)S(1)}, bf16[4,256,1344]{1,2,0:T(8,128)(2,1)}, u32[]{:S(2)}, u32[]{:S(2)}) collective-permute-start(bf16[4,256,1344]{1,2,0:T(8,128)(2,1)S(1)} %copy.75), channel_id=1, source_target_pairs={{0,16},{16,0},{1,17},{17,1},{2,18},{18,2},{3,19},{19,3},{4,20},{20... | collective-permute-start | bytes 8257544 | tf_op jit(solution)/shard_map/ppermute | solution.py:126
  536.1 50.9 %copy-start.10 = (bf16[512,2048]{0,1:T(8,128)(2,1)S(1)}, bf16[512,2048]{0,1:T(8,128)(2,1)}, u32[]{:S(2)}) copy-start(bf16[512,2048]{0,1:T(8,128)(2,1)} %all-gather.18.cloned.1.call-done) | copy-start | bytes 6291460
  543.3 54.7 %copy-start.7 = (f32[1344]{0:T(1024)S(1)}, f32[1344]{0:T(1024)}, u32[]{:S(2)}) copy-start(f32[1344]{0:T(1024)} %param.17) | copy-start | bytes 16132
  587.0 14.8 %copy-start.1 = (bf16[1024,1344]{0,1:T(8,128)(2,1)S(1)}, bf16[1024,1344]{0,1:T(8,128)(2,1)}, u32[]{:S(2)}) copy-start(bf16[1024,1344]{0,1:T(8,128)(2,1)} %param.16) | copy-start | bytes 8257540
  (1 other events, 2.0 us)
Sparse Core Ops, SparseCore 0:
  8.9 56.6 all-gather.21
  67.2 100.6 all-gather.23
  169.4 55.6 all-gather.19
  226.5 40.9 all-gather.13
  269.0 119.5 all-gather.25
  390.0 82.8 all-gather.27
  474.4 33.1 all-gather.17
  510.3 21.6 all-gather.15
